TPU v7x, 32 devices: a whole 2x2x4 slice. The times are simulated.
32 devices in a mesh: groups: 2 (over y), wide: 8 (over z, x), short: 2 (over core).
Axes of the slice: x: 2, y: 2, z: 4, core: 2. Of those that a mesh axis runs over, the one named last changes fastest.
Arguments:
- tokens: bfloat16 [64, 5120], P(('groups', 'wide'), 'short'), parts along dimension 0, may hold values from -6 to 6
- norm_gain: float32 [5120], P('short'), may hold values from 0.5 to 1.5
- mixer_in: bfloat16 [5120, 2, 5888], P('short', None, 'wide'), may hold values from -0.078125 to 0.078125
- shared_in: bfloat16 [5120, 512], P('short', 'wide'), may hold values from -0.078125 to 0.078125
- step_in: bfloat16 [5120, 32], P('short'), may hold values from -0.078125 to 0.078125
- step_bias: float32 [32], P('short'), may hold values from -2 to 1
- decay_rate: float32 [32], P('short'), may hold values from 0.05 to 4
- skip_gain: float32 [32], P('short'), may hold values from 0.2 to 1.5
- cached_keys: bfloat16 [16, 512, 512], P(('groups', 'wide'), None, 'short'), parts along dimension 0, may hold values from -64 to 64
- cached_values: bfloat16 [16, 512, 512], P(('groups', 'wide'), None, 'short'), parts along dimension 0, may hold values from -6 to 6
- lengths: int32 [16], P(('groups', 'wide')), parts along dimension 0, may hold values from 2 to 512, as said below
- state_cache: bfloat16 [16, 32, 128, 256], P(('groups', 'wide'), 'short'), parts along dimension 0, may hold values from -6 to 6
- mixer_gain: float32 [4096], P('short'), may hold values from 0.5 to 1.5
- mixer_out: bfloat16 [2, 3328, 5120], P(None, 'wide', 'short'), may hold values from -0.078125 to 0.078125
- gate_weight: bfloat16 [5120, 21504], P('short', 'wide'), may hold values from -0.078125 to 0.078125
- up_weight: bfloat16 [5120, 21504], P('short', 'wide'), may hold values from -0.078125 to 0.078125
- down_weight: bfloat16 [21504, 5120], P('wide', 'short'), may hold values from -0.0390625 to 0.0390625
Outputs:
- mixed: bfloat16 [64, 5120], P(('groups', 'wide'), 'short'), parts along dimension 0
There are 2 independent parts, one for each index of `groups`. A program takes and returns all parts, laid end to end along the dimension named above; an argument that names none is the same for every part. Nothing has to cross between parts.
Inputs may be any that keep to these rules, and one draw needn't show every extreme that they name: `lengths`: in every draw some request holds exactly 512 earlier tokens.
All inputs are finite; a program needn't handle non-finite values.
Results may differ from a plain program's by a relative error of at most 0.009.
Values may be sent and summed in bfloat16 or wider, within the bound.
A program may use at most 128 MiB of HBM per device.

v0:
```python
import jax
import jax.numpy as jnp
from jax import lax
from jax.sharding import PartitionSpec as P

D = 5120
QUERY_HEADS = 20
KEY_VALUE_HEADS = 4
HEAD_SIZE = 128
MH = 32
MP = 128
NS = 256
CACHE_SLOTS = 512
DRAFT_TOKENS = 4


epsilon = 1e-05


def as_sent(x):

    def short(part):
        return part.astype(jnp.bfloat16) if part.dtype == jnp.float32 else part

    return jax.tree.map(short, x)


def rotate(vectors, cos_table, sin_table):
    half_width = vectors.shape[-1] // 2
    first_half = vectors[..., :half_width]
    second_half = vectors[..., half_width:]
    return jnp.concatenate(
        [
            first_half * cos_table - second_half * sin_table,
            second_half * cos_table + first_half * sin_table,
        ],
        axis=-1,
    )


def rope_tables(positions):
    frequency = 10000.0 ** (-(jnp.arange(HEAD_SIZE // 2, dtype=jnp.float32) * 2.0 / HEAD_SIZE))
    angles = positions.astype(jnp.float32)[..., None] * frequency
    return (jnp.cos(angles), jnp.sin(angles))


def attend_one(queries, fresh_keys, fresh_values, key_tile_block, value_tile_block, length):
    score_scale = HEAD_SIZE ** (-0.5)
    scores_cache = (
        jnp.einsum("tkgd,pkd->kgtp", queries, key_tile_block, preferred_element_type=jnp.float32)
        * score_scale
    )
    scores_new = (
        jnp.einsum("tkgd,ukd->kgtu", queries, fresh_keys, preferred_element_type=jnp.float32)
        * score_scale
    )
    live_keys = jnp.arange(key_tile_block.shape[0], dtype=jnp.int32) < length
    causal = jnp.arange(DRAFT_TOKENS)[None, :] <= jnp.arange(DRAFT_TOKENS)[:, None]
    scores_cache = jnp.where(live_keys, scores_cache, -1e30)
    scores_new = jnp.where(causal, scores_new, -1e30)
    highest = jnp.maximum(jnp.max(scores_cache, axis=-1), jnp.max(scores_new, axis=-1))[..., None]
    weight_cache = jnp.exp(scores_cache - highest)
    weight_new = jnp.exp(scores_new - highest)
    denominator = jnp.sum(weight_cache, axis=-1, keepdims=True) + jnp.sum(
        weight_new, axis=-1, keepdims=True
    )
    probs_cache = (weight_cache / denominator).astype(jnp.bfloat16)
    probs_new = (weight_new / denominator).astype(jnp.bfloat16)
    attended = jnp.einsum(
        "kgtp,pkd->tkgd", probs_cache, value_tile_block, preferred_element_type=jnp.float32
    )
    attended = attended + jnp.einsum(
        "kgtu,ukd->tkgd", probs_new, fresh_values, preferred_element_type=jnp.float32
    )
    return attended.astype(jnp.bfloat16)


def scan_one(
    state_block, inputs_x, gates_z, b_vals, c_vals, step_sizes, decay_rates, skip_gain, head_gain
):
    hstate = state_block.astype(jnp.float32)
    in_active = jax.nn.silu(inputs_x.astype(jnp.float32))
    write_vec = jax.nn.silu(b_vals.astype(jnp.float32))
    read_vec = jax.nn.silu(c_vals.astype(jnp.float32))
    outputs = []
    for draft_index in range(DRAFT_TOKENS):
        decays = jnp.exp(-step_sizes[draft_index] * decay_rates)
        inject = (step_sizes[draft_index][:, None] * in_active[draft_index])[
            :, :, None
        ] * write_vec[draft_index][None, None, :]
        hstate = decays[:, None, None] * hstate + inject
        readout = jnp.einsum(
            "hpn,n->hp", hstate, read_vec[draft_index], precision=lax.Precision.HIGHEST
        )
        outputs.append(readout + skip_gain[:, None] * in_active[draft_index])
    gated = jnp.stack(outputs) * jax.nn.silu(gates_z.astype(jnp.float32))
    mean_square = jnp.mean(gated * gated, axis=-1, keepdims=True)
    return (gated * lax.rsqrt(mean_square + epsilon) * head_gain).astype(jnp.bfloat16)


def on_device(
    tokens,
    norm_gain,
    mixer_in,
    shared_in,
    step_in,
    step_bias,
    decay_rate,
    skip_gain,
    cached_keys,
    cached_values,
    lengths,
    state_cache,
    mixer_gain,
    mixer_out,
    gate_weight,
    up_weight,
    down_weight,
):
    short_count = lax.axis_size("short")
    n_wide = lax.axis_size("wide")
    q_heads = QUERY_HEADS // short_count
    key_value_heads = KEY_VALUE_HEADS // short_count
    ssm_heads = MH // short_count
    repeat_factor = QUERY_HEADS // KEY_VALUE_HEADS
    query_size = q_heads * HEAD_SIZE
    key_size = key_value_heads * HEAD_SIZE
    m_size = ssm_heads * MP
    local_rows = tokens.shape[0]
    requests = local_rows // DRAFT_TOKENS
    width_half = tokens.shape[1]
    rows_float = tokens.astype(jnp.float32)
    square_sum = lax.psum(jnp.sum(rows_float * rows_float, axis=1), "short")
    inv_rms = lax.rsqrt(square_sum / D + epsilon)
    normed = (rows_float * inv_rms[:, None] * norm_gain[None, :]).astype(jnp.bfloat16)
    step_terms = jnp.dot(normed, step_in, preferred_element_type=jnp.float32)
    step_raw = lax.psum_scatter(step_terms, "short", scatter_dimension=1, tiled=True)
    gathered = lax.all_gather(normed, "wide", axis=0, tiled=True)
    group_part = jnp.einsum("rd,dgc->rgc", gathered, mixer_in, preferred_element_type=jnp.float32)
    shared_part = jnp.dot(gathered, shared_in, preferred_element_type=jnp.float32)[:, None, :]
    gate_part = jnp.dot(gathered, gate_weight, preferred_element_type=jnp.float32)
    up_part = jnp.dot(gathered, up_weight, preferred_element_type=jnp.float32)
    gate_half, up_half = (
        lax.psum_scatter(
            gate_part.astype(jnp.bfloat16), "short", scatter_dimension=0, tiled=True
        ).astype(jnp.float32),
        lax.psum_scatter(
            up_part.astype(jnp.bfloat16), "short", scatter_dimension=0, tiled=True
        ).astype(jnp.float32),
    )
    hidden_half = (jax.nn.silu(gate_half) * up_half).astype(jnp.bfloat16)
    hidden = lax.all_gather(hidden_half, "short", axis=0, tiled=True)
    group_moved, shared_moved = (
        lax.all_to_all(group_part, "wide", split_axis=0, concat_axis=2, tiled=True),
        lax.all_to_all(shared_part, "wide", split_axis=0, concat_axis=2, tiled=True),
    )
    group_sum = lax.psum_scatter(group_moved, "short", scatter_dimension=1, tiled=True)
    shared_sum = lax.psum(shared_moved, "short")
    features = group_sum[:, 0, :].astype(jnp.bfloat16)
    shared_vals = shared_sum[:, 0, :].astype(jnp.bfloat16)
    queries = features[:, :query_size].reshape(requests, DRAFT_TOKENS, q_heads, HEAD_SIZE)
    fresh_keys = features[:, query_size : query_size + key_size].reshape(
        requests, DRAFT_TOKENS, key_value_heads, HEAD_SIZE
    )
    fresh_values = features[:, query_size + key_size : query_size + 2 * key_size].reshape(
        requests, DRAFT_TOKENS, key_value_heads, HEAD_SIZE
    )
    x_start = query_size + 2 * key_size
    inputs_x = features[:, x_start : x_start + m_size].reshape(
        requests, DRAFT_TOKENS, ssm_heads, MP
    )
    gates_z = features[:, x_start + m_size : x_start + 2 * m_size].reshape(
        requests, DRAFT_TOKENS, ssm_heads, MP
    )
    positions = lengths[:, None] + jnp.arange(DRAFT_TOKENS, dtype=jnp.int32)[None, :]
    cos_table, sin_table = rope_tables(positions)
    cos_table = cos_table[:, :, None, :]
    sin_table = sin_table[:, :, None, :]
    rotated_queries = rotate(queries.astype(jnp.float32), cos_table, sin_table).astype(jnp.bfloat16)
    keys_rot = rotate(fresh_keys.astype(jnp.float32), cos_table, sin_table).astype(jnp.bfloat16)
    rotated_queries = rotated_queries.reshape(
        requests, DRAFT_TOKENS, key_value_heads, repeat_factor, HEAD_SIZE
    )
    key_tile_block = cached_keys.reshape(requests, CACHE_SLOTS, key_value_heads, HEAD_SIZE)
    value_tile_block = cached_values.reshape(requests, CACHE_SLOTS, key_value_heads, HEAD_SIZE)
    attention = jax.vmap(attend_one)(
        rotated_queries, keys_rot, fresh_values, key_tile_block, value_tile_block, lengths
    )
    step_sizes = jax.nn.softplus(
        step_raw.reshape(requests, DRAFT_TOKENS, ssm_heads) + step_bias[None, None, :]
    )
    b_vals = shared_vals[:, :NS].reshape(requests, DRAFT_TOKENS, NS)
    c_vals = shared_vals[:, NS:].reshape(requests, DRAFT_TOKENS, NS)
    head_gain = mixer_gain.reshape(ssm_heads, MP)
    mamba = jax.vmap(scan_one, in_axes=(0, 0, 0, 0, 0, 0, None, None, None))(
        state_cache, inputs_x, gates_z, b_vals, c_vals, step_sizes, decay_rate, skip_gain, head_gain
    )
    own_rows = jnp.concatenate(
        [attention.reshape(local_rows, query_size), mamba.reshape(local_rows, m_size)], axis=1
    )
    returned = lax.all_to_all(
        as_sent(own_rows[:, None, :]), "wide", split_axis=2, concat_axis=0, tiled=True
    )
    both_groups = lax.all_gather(as_sent(returned), "short", axis=1, tiled=True).astype(
        returned.dtype
    )
    projected = jnp.einsum(
        "rgc,gcd->rd", both_groups, mixer_out, preferred_element_type=jnp.float32
    )
    summed = projected + jnp.dot(hidden, down_weight, preferred_element_type=jnp.float32)
    pieces = lax.all_to_all(
        summed.reshape(n_wide, local_rows, width_half).astype(jnp.bfloat16),
        "wide",
        split_axis=0,
        concat_axis=0,
        tiled=True,
    ).astype(jnp.float32)
    total = rows_float + jnp.sum(pieces, axis=0)
    return total.astype(jnp.bfloat16)


def solution(mesh):
    in_specs = (
        P(("groups", "wide"), "short"),
        P("short"),
        P("short", None, "wide"),
        P("short", "wide"),
        P("short", None),
        P("short"),
        P("short"),
        P("short"),
        P(("groups", "wide"), None, "short"),
        P(("groups", "wide"), None, "short"),
        P(("groups", "wide")),
        P(("groups", "wide"), "short", None, None),
        P("short"),
        P(None, "wide", "short"),
        P("short", "wide"),
        P("short", "wide"),
        P("wide", "short"),
    )
    out_specs = P(("groups", "wide"), "short")
    return jax.shard_map(
        on_device, mesh=mesh, in_specs=in_specs, out_specs=out_specs, check_vma=False
    )
```

profile of v0, /device:TPU:0, one launch (start us, length us, event | category | flops | bytes accessed | tf_op | source)
XLA Modules:
  0.0 175.8 jit_solution(5876749389254881673)
XLA Ops:
  6.5 0.9 fusion.60
  7.4 2.6 %psum.14 = f32[4]{0:T(128)S(1)} all-reduce(f32[4]{0:T(128)S(1)} %fusion.60), channel_id=1, replica_groups=mesh['groups'=2,'wide'=8,'short'=2] {'short'}, use_global_device_ids=true, to_apply=%region_1.0 | all-reduce | flops 4 | bytes 32 | tf_op jit(solution)/shard_map/psum | solution.py:133
  10.1 0.8 fusion.99
  10.9 32.2 %all-gather = bf16[8,4,2560]{2,1,0:T(4,128)(2,1)S(1)} all-gather(bf16[1,4,2560]{2,1,0:T(4,128)(2,1)S(1)} %fusion.99), channel_id=1, replica_groups=mesh['groups'=2,'wide'=8,'short'=2] {'wide'}, dimensions={0}, use_global_device_ids=true | all-gather | bytes 184320 | tf_op jit(solution)/shard_map/all_gather | solution.py:138
  43.2 0.2 fusion.104
  43.4 0.6 broadcast.301
  44.0 0.7 reduce.5
  44.7 0.7 reshape.648
  45.3 5.5 %all-to-all-start.1 = ((f32[8,1,256]{2,1,0:T(1,128)}), f32[8,1,256]{2,1,0:T(1,128)S(1)}, u32[]{:S(2)}, u32[]{:S(2)}) async-start(f32[8,1,256]{2,1,0:T(1,128)} %reshape.648), calls=%async_computation.1 | async-start | bytes 16384 | tf_op jit(solution)/shard_map/all_to_all | solution.py:155
  50.8 1.8 %convolution_bitcast_fusion.2 = f32[32,4]{1,0:T(8,128)} fusion(bf16[2560,32]{0,1:T(8,128)(2,1)} %param.21, bf16[4,2560]{1,0:T(4,128)(2,1)} %param.17, f32[2560]{0:T(1024)} %param.18, f32[4]{0:T(128)S(1)} %add_rsqrt_fusion.1), kind=kOutput, calls=%fused_computation.27 | convolution fusion | flops 696320 | bytes 195088
  52.7 8.0 %convolution_convert_fusion.1 = bf16[32,2688]{1,0:T(8,128)(2,1)} fusion(bf16[32,2560]{1,0:T(8,128)(2,1)S(1)} %reshape.629, bf16[2560,2688]{1,0:T(8,128)(2,1)} %param.31), kind=kOutput, calls=%fused_computation.4 | convolution fusion | flops 440487936 | bytes 14098432 | tf_op jit(solution)/shard_map/dot_general | solution.py:141
  60.8 8.0 %convolution_convert_fusion = bf16[32,2688]{1,0:T(8,128)(2,1)} fusion(bf16[32,2560]{1,0:T(8,128)(2,1)S(1)} %reshape.629, bf16[2560,2688]{1,0:T(8,128)(2,1)} %param.32), kind=kOutput, calls=%fused_computation.3 | convolution fusion | flops 440487936 | bytes 14098432 | tf_op jit(solution)/shard_map/dot_general | solution.py:142
  69.0 5.4 %fusion.103 = f32[32,2,736]{2,0,1:T(8,128)S(1)} fusion(bf16[32,2560,1]{1,0,2:T(8,128)(2,1)S(1)} %reshape.630, bf16[2560,2,736]{0,2,1:T(8,128)(2,1)} %param.19), kind=kOutput, calls=%fused_computation.182 | convolution fusion | flops 241172480 | bytes 7888896 | tf_op jit(solution)/shard_map/rd,dgc->rgc/dot_general | solution.py:139
  74.4 0.8 copy.63
  76.1 0.6 dynamic-slice
  76.6 0.1 multiply_cosine_fusion
  76.8 0.8 copy.94
  77.6 6.1 %all-to-all-start = ((f32[32,2,736]{2,1,0:T(2,128)}), f32[32,2,736]{2,1,0:T(2,128)S(1)}, u32[]{:S(2)}, u32[]{:S(2)}) async-start(f32[32,2,736]{2,1,0:T(2,128)} %copy.63), calls=%async_computation | async-start | bytes 393216 | tf_op jit(solution)/shard_map/all_to_all | solution.py:154
  83.7 0.7 reduce.6
  84.6 6.9 %all-to-all-done = f32[32,2,736]{2,1,0:T(2,128)S(1)} async-done(((f32[32,2,736]{2,1,0:T(2,128)}), f32[32,2,736]{2,1,0:T(2,128)S(1)}, u32[]{:S(2)}, u32[]{:S(2)}) %all-to-all-start) | async-done | bytes 188448 | tf_op jit(solution)/shard_map/all_to_all | solution.py:154
  91.6 0.3 all_to_all.45
  91.9 4.2 %all-reduce.3 = (bf16[4,2,5888]{2,0,1:T(4,128)(2,1)S(1)}, bf16[4,1,512]{2,0,1:T(4,128)(2,1)S(1)}) all-reduce(f32[4,2,5888]{2,0,1:T(4,128)S(1)} %copy.65, f32[4,1,512]{2,0,1:T(4,128)S(1)} %all_to_all.49), channel_id=2, replica_groups=mesh['groups'=2,'wide'=8,'short'=2] {'short'}, use_global_device_ids=true, to_apply=%region_2.0.clone | all-reduce | flops 49152 | bytes 294912
  96.0 0.6 fusion.59
  96.9 0.3 fusion.101
  97.2 0.3 fusion.102
  97.5 0.2 fusion.56
  97.7 0.2 convolution_bitcast_fusion.1
  98.0 0.2 fusion.16
  98.4 2.2 %fusion.7 = f32[1,16,128]{2,0,1:T(1,128)S(1)} fusion(bf16[1,16,128,256]{3,2,1,0:T(8,128)(2,1)S(1)} %copy-done.8, f32[256]{0:T(256)S(1)} %bitcast.286, f32[16,128]{1,0:T(8,128)S(1)} %get-tuple-element.15, f32[16]{0:T(128)S(1)} %get-tuple-element.27, f32[1,4,256]{2,1,0:T(4,128)S(1)} %get-tuple-element.21), kind=kOutput, calls=%fused_computation.11 | convolution fusion | flops 8388608 | bytes 1067520 | tf_op jit(solution)/shard_map/vmap(hpn,n->hp)/dot_general | solution.py:92
  100.5 2.6 %fusion.5 = f32[1,16,128]{2,0,1:T(1,128)S(1)} fusion(bf16[1,16,128,256]{3,2,1,0:T(8,128)(2,1)S(1)} %copy-done.8, f32[256]{0:T(256)S(1)} %bitcast.293, f32[16,128]{1,0:T(8,128)S(1)} %get-tuple-element.18, f32[16]{0:T(128)S(1)} %get-tuple-element.28, f32[256]{0:T(256)S(1)} %bitcast.287, f32[16,128]{1,0:T(8,128)S(1)} %get-tuple-element.15, ...), kind=kOutput, calls=%fused_computation.9 | convolution fusion | flops 9961472 | bytes 1077248 | tf_op jit(solution)/shard_map/vmap(hpn,n->hp)/dot_general | solution.py:92
  103.1 2.8 %fusion.3 = f32[1,16,128]{2,0,1:T(1,128)S(1)} fusion(bf16[1,16,128,256]{3,2,1,0:T(8,128)(2,1)S(1)} %copy-done.8, f32[256]{0:T(256)S(1)} %bitcast.291, f32[16,128]{1,0:T(8,128)S(1)} %get-tuple-element.17, f32[16]{0:T(128)S(1)} %get-tuple-element.30, f32[256]{0:T(256)S(1)} %bitcast.294, f32[16,128]{1,0:T(8,128)S(1)} %get-tuple-element.18, ...), kind=kOutput, calls=%fused_computation.7 | convolution fusion | flops 11534336 | bytes 1086976 | tf_op jit(solution)/shard_map/vmap(hpn,n->hp)/dot_general | solution.py:92
  105.9 3.0 %fusion.1 = f32[1,16,128]{2,0,1:T(1,128)S(1)} fusion(bf16[1,16,128,256]{3,2,1,0:T(8,128)(2,1)S(1)} %copy-done.8, f32[256]{0:T(256)S(1)} %bitcast.290, f32[16,128]{1,0:T(8,128)S(1)} %get-tuple-element.16, f32[16]{0:T(128)S(1)} %get-tuple-element.29, f32[256]{0:T(256)S(1)} %bitcast.292, f32[16,128]{1,0:T(8,128)S(1)} %get-tuple-element.17, ...), kind=kOutput, calls=%fused_computation.5 | convolution fusion | flops 13107200 | bytes 1096704 | tf_op jit(solution)/shard_map/vmap(hpn,n->hp)/dot_general | solution.py:92
  109.3 2.4 %copy.78 = bf16[4,1,3328]{0,1,2:T(2,128)(2,1)S(1)} copy(bf16[4,1,3328]{2,0,1:T(4,128)(2,1)S(1)} %maximum_bitcast_fusion.1) | data formatting | bytes 53248 | tf_op jit(solution)/shard_map/broadcast_in_dim | solution.py:202
  111.7 0.5 broadcast.303
  112.2 18.3 %reduce.7 = bf16[3328,4]{1,0:T(8,128)(2,1)S(1)} reduce(bf16[3328,1,4]{2,1,0:T(2,128)(2,1)S(1)} %bitcast.260, bf16[]{:T(256)} %broadcast.303), dimensions={1}, to_apply=%bitcast.239.reduce_sub_computation | reduce | bytes 53250
  130.5 1.4 reshape.650
  131.9 3.3 %all-to-all-start.2 = ((bf16[8,2,832]{2,1,0:T(2,128)(2,1)}), bf16[8,2,832]{2,1,0:T(2,128)(2,1)S(1)}, u32[]{:S(2)}, u32[]{:S(2)}) async-start(bf16[8,2,832]{2,1,0:T(2,128)(2,1)} %reshape.650), calls=%async_computation.2 | async-start | bytes 57344 | tf_op jit(solution)/shard_map/all_to_all | solution.py:201
  135.3 1.0 fusion.55
  136.3 2.1 %all_gather.11 = bf16[32,2688]{1,0:T(8,128)(2,1)S(1)} all-gather(bf16[16,2688]{1,0:T(8,128)(2,1)S(1)} %fusion.55), channel_id=1, replica_groups=mesh['groups'=2,'wide'=8,'short'=2] {'short'}, dimensions={0}, use_global_device_ids=true | all-gather | bytes 258048 | tf_op jit(solution)/shard_map/all_gather | solution.py:152
  138.5 3.4 %all-to-all-done.2 = bf16[8,2,832]{2,1,0:T(2,128)(2,1)S(1)} async-done(((bf16[8,2,832]{2,1,0:T(2,128)(2,1)}), bf16[8,2,832]{2,1,0:T(2,128)(2,1)S(1)}, u32[]{:S(2)}, u32[]{:S(2)}) %all-to-all-start.2) | async-done | bytes 26656 | tf_op jit(solution)/shard_map/all_to_all | solution.py:201
  141.9 2.1 %reshape.651 = bf16[3328,1,4]{2,1,0:T(2,128)(2,1)S(1)} reshape(bf16[8,2,832]{2,1,0:T(2,128)(2,1)S(1)} %all-to-all-done.2) | data formatting | bytes 53248
  143.9 1.7 copy.79
  145.6 0.1 all_to_all.51
  145.8 1.9 %all_gather.10 = bf16[32,2,416]{2,0,1:T(8,128)(2,1)S(1)} all-gather(bf16[32,1,416]{2,0,1:T(8,128)(2,1)S(1)} %all_to_all.53), channel_id=1, replica_groups=mesh['groups'=2,'wide'=8,'short'=2] {'short'}, dimensions={1}, use_global_device_ids=true | all-gather | bytes 79872 | tf_op jit(solution)/shard_map/all_gather | solution.py:204
  147.6 3.0 %convolution_bitcast_fusion = f32[32,2560]{1,0:T(8,128)S(1)} fusion(bf16[32,2,416]{2,0,1:T(8,128)(2,1)S(1)} %all_gather.10, bf16[2,416,2560]{2,1,0:T(8,128)(2,1)} %param.30), kind=kOutput, calls=%fused_computation.1 | convolution fusion | flops 136314880 | bytes 4640768 | tf_op jit(solution)/shard_map/rgc,gcd->rd/dot_general | solution.py:207
  150.6 7.4 %fusion = bf16[32,2560]{1,0:T(8,128)(2,1)S(1)} fusion(f32[32,2560]{1,0:T(8,128)S(1)} %convolution_bitcast_fusion, bf16[32,2688]{1,0:T(8,128)(2,1)S(1)} %all_gather.11, bf16[2688,2560]{1,0:T(8,128)(2,1)} %param.33), kind=kOutput, calls=%fused_computation.2 | convolution fusion | flops 440565760 | bytes 14426112 | tf_op jit(solution)/shard_map/dot_general | solution.py:210
  158.1 10.5 %all_to_all.59 = bf16[8,4,2560]{2,1,0:T(4,128)(2,1)S(1)} all-to-all(bf16[8,4,2560]{2,1,0:T(4,128)(2,1)S(1)} %convert_element_type.187), channel_id=1, replica_groups=mesh['groups'=2,'wide'=8,'short'=2] {'wide'}, dimensions={0} | all-to-all | bytes 327680 | tf_op jit(solution)/shard_map/all_to_all | solution.py:211
  168.6 0.6 fusion.63
  (76 shorter events, 1.8 us)
Async XLA Ops:
  6.5 36.7 %copy-start = (bf16[2560,64]{0,1:T(8,128)(2,1)S(1)}, bf16[2560,64]{0,1:T(8,128)(2,1)}, u32[]{:S(2)}) copy-start(bf16[2560,64]{0,1:T(8,128)(2,1)} %param.20) | copy-start | bytes 983044
  45.3 32.2 %all-to-all-start.1 = ((f32[8,1,256]{2,1,0:T(1,128)}), f32[8,1,256]{2,1,0:T(1,128)S(1)}, u32[]{:S(2)}, u32[]{:S(2)}) async-start(f32[8,1,256]{2,1,0:T(1,128)} %reshape.648), calls=%async_computation.1 | async-start | bytes 16384 | tf_op jit(solution)/shard_map/all_to_all | solution.py:155
  50.8 26.0 %reduce-scatter.10.cloned.1.call-start = ((), (), s32[]{:S(2)}) async-start(), calls=%async_computation.9 | async-start | bytes 24576
  52.7 82.6 %reduce-scatter.6.cloned.1.call-start = ((), (), s32[]{:S(2)}) async-start(), calls=%async_computation.7 | async-start | bytes 258048 | tf_op jit(solution)/shard_map/reduce_scatter | solution.py:144
  60.8 74.5 %reduce-scatter.8.cloned.1.call-start = ((), (), s32[]{:S(2)}) async-start(), calls=%async_computation.8 | async-start | bytes 258048 | tf_op jit(solution)/shard_map/reduce_scatter | solution.py:147
  69.0 6.9 %copy-start.1 = (bf16[1,512,256]{2,1,0:T(8,128)(2,1)S(1)}, bf16[1,512,256]{2,1,0:T(8,128)(2,1)}, u32[]{:S(2)}) copy-start(bf16[1,512,256]{2,1,0:T(8,128)(2,1)} %param.25) | copy-start | bytes 786436
  69.0 7.0 %copy-start.2 = (bf16[1,512,256]{2,1,0:T(8,128)(2,1)S(1)}, bf16[1,512,256]{2,1,0:T(8,128)(2,1)}, u32[]{:S(2)}) copy-start(bf16[1,512,256]{2,1,0:T(8,128)(2,1)} %param.26) | copy-start | bytes 786436
  69.0 7.1 %copy-start.9 = (u32[32]{0:T(128)S(1)}, u32[32]{0:T(128)}, u32[]{:S(2)}) copy-start(u32[32]{0:T(128)} %constant.43) | copy-start | bytes 388
  69.0 8.5 %copy-start.6 = (f32[16]{0:T(128)S(1)}, f32[16]{0:T(128)}, u32[]{:S(2)}) copy-start(f32[16]{0:T(128)} %param.22) | copy-start | bytes 196
  69.0 14.7 %copy-start.7 = (f32[16]{0:T(128)S(1)}, f32[16]{0:T(128)}, u32[]{:S(2)}) copy-start(f32[16]{0:T(128)} %param.23) | copy-start | bytes 196
  77.6 20.8 %copy-start.8 = (bf16[1,16,128,256]{3,2,1,0:T(8,128)(2,1)S(1)}, bf16[1,16,128,256]{3,2,1,0:T(8,128)(2,1)}, u32[]{:S(2)}) copy-start(bf16[1,16,128,256]{3,2,1,0:T(8,128)(2,1)} %param.28) | copy-start | bytes 3145732
  77.6 13.9 %all-to-all-start = ((f32[32,2,736]{2,1,0:T(2,128)}), f32[32,2,736]{2,1,0:T(2,128)S(1)}, u32[]{:S(2)}, u32[]{:S(2)}) async-start(f32[32,2,736]{2,1,0:T(2,128)} %copy.63), calls=%async_computation | async-start | bytes 393216 | tf_op jit(solution)/shard_map/all_to_all | solution.py:154
  105.9 3.0 %copy-start.5 = (f32[16]{0:T(128)S(1)}, f32[16]{0:T(128)}, u32[]{:S(2)}) copy-start(f32[16]{0:T(128)} %param.24) | copy-start | bytes 196
  105.9 3.3 %copy-start.4 = (f32[2048]{0:T(1024)S(1)}, f32[2048]{0:T(1024)}, u32[]{:S(2)}) copy-start(f32[2048]{0:T(1024)} %param.29) | copy-start | bytes 24580
  131.9 9.9 %all-to-all-start.2 = ((bf16[8,2,832]{2,1,0:T(2,128)(2,1)}), bf16[8,2,832]{2,1,0:T(2,128)(2,1)S(1)}, u32[]{:S(2)}, u32[]{:S(2)}) async-start(bf16[8,2,832]{2,1,0:T(2,128)(2,1)} %reshape.650), calls=%async_computation.2 | async-start | bytes 57344 | tf_op jit(solution)/shard_map/all_to_all | solution.py:201
  150.6 18.0 %copy-start.3 = (bf16[4,2560]{1,0:T(4,128)(2,1)S(1)}, bf16[4,2560]{1,0:T(4,128)(2,1)}, u32[]{:S(2)}) copy-start(bf16[4,2560]{1,0:T(4,128)(2,1)} %param.17) | copy-start | bytes 61444
Sparse Core Ops, SparseCore 0:
  53.8 8.9 reduce-scatter.9
  65.0 8.7 reduce-scatter.5
  76.0 8.7 reduce-scatter.7
where the time goes:
time: 177 us; the launch traced here: 176 us
  blocking collectives  53.5 us (30%)
  matrix products  45.4 us (26%)
  other arithmetic  24.1 us (14%)
  starting transfers between devices  15 us (8%)
  between operations  14.2 us (8%)
  local copies, waits for them, and re-layouts  13.2 us (7%)
  waiting for transfers between devices  10.4 us (6%)
    all_gather x1, blocking collectives, on_device(): gathered = lax.all_gather(normed, 'wide', axis=0, tiled=True)  32.2 us
    unnamed x3, other arithmetic  19.2 us
    dot_general x4, matrix products, scan_one(): jnp.einsum('hpn,n->hp', hstate, read_vec[draft_index], precision=lax.Prec...  10.6 us
    all_to_all x1, blocking collectives, on_device(): lax.all_to_all(summed.reshape(n_wide, local_rows, width_half).astype(jnp....  10.5 us
    dot_general x1, matrix products, on_device(): up_part = jnp.dot(gathered, up_weight, preferred_element_type=jnp.float32)  8.04 us
    dot_general x1, matrix products, on_device(): jnp.dot(gathered, gate_weight, preferred_element_type=jnp.float32)  8.02 us
    dot_general x1, matrix products, on_device(): jnp.dot(hidden, down_weight, preferred_element_type=jnp.float32)  7.37 us
    all_to_all x1, waiting for transfers between devices, on_device(): lax.all_to_all(group_part, 'wide', split_axis=0, concat_axis=2, tiled=True)  6.92 us
  transfers between devices with their start and end apart: 6, of which 2 were waited for; matrix products, arithmetic and copies ran while one was open for 36% of the time, Pallas kernels for 0%

commit v1 on v0

--- a/solution.py
+++ b/solution.py
@@ -1,6 +1,9 @@
+import functools
 import jax
 import jax.numpy as jnp
 from jax import lax
+from jax.experimental import pallas as pl
+from jax.experimental.pallas import tpu as pltpu
 from jax.sharding import PartitionSpec as P
 
 D = 5120
@@ -219,6 +222,469 @@
     return total.astype(jnp.bfloat16)
 
 
+MESH = pl.DeviceIdType.MESH
+F32 = jnp.float32
+BF16 = jnp.bfloat16
+NT = (((1,), (1,)), ((), ()))
+LANE = 128
+
+
+def silu(v):
+    return v / (1.0 + jnp.exp(-v))
+
+
+def dot(a, b):
+    return jnp.dot(a, b, preferred_element_type=F32)
+
+
+def dot_nt(a, b):
+    return lax.dot_general(a, b, NT, preferred_element_type=F32)
+
+
+def fused_kernel(
+    dims,
+    tokens, gain, bias, rate, skip, lengths, cosf, sinf, mixer_gain,
+    mixer_in, shared_in, step_in, keys, values, state, mixer_out, gate, up, down,
+    out,
+    w_a, w_b, k_v, v_v, s_v, g_v, u_v, m_v, d_v,
+    xg, xf, xb, sq_send, sq_recv, p_send, p_recv, c_b, tot, step_f,
+    f_send, f_recv, feat, bc, qbuf, knbuf, vnbuf, obuf, cbuf, rbuf, own,
+    m_send, m_recv, lhs, gsc, gu_send, gu_recv, hbuf, o_send, o_recv,
+    sem_w, sem_loc, sem_gs, sem_gr, sem_ps, sem_pr, sem_fs, sem_fr,
+    sem_ms, sem_mr, sem_us, sem_ur, sem_hs, sem_hr, sem_os, sem_or,
+):
+    n, n_short, rows, width, gcol, scol, ncol, ocol, n_chunk, fchunk, n_oc, ochunk = dims
+    total_rows = n * rows
+    me = lax.axis_index("wide")
+    s = lax.axis_index("short")
+    other = 1 - s
+    q_heads = QUERY_HEADS // n_short
+    kv_heads = KEY_VALUE_HEADS // n_short
+    m_heads = MH // n_short
+    rep = QUERY_HEADS // KEY_VALUE_HEADS
+    acol = gcol + scol + ncol
+    fpad = xpad(gcol)
+    opad = round_up(ocol)
+
+    def peer(d):
+        return lax.rem(me + d, n)
+
+    weights = []
+
+    def fetch(src, dst):
+        copy = pltpu.make_async_copy(src, dst, sem_w.at[len(weights)])
+        copy.start()
+        weights.append(copy)
+        return copy
+
+    fa = [
+        fetch(mixer_in.at[other], w_a.at[pl.ds(0, gcol)]),
+        fetch(shared_in, w_a.at[pl.ds(gcol, scol)]),
+        fetch(step_in, w_a.at[pl.ds(gcol + scol, ncol)]),
+    ]
+    fb = [fetch(mixer_in.at[s], w_b)]
+
+    barrier = pltpu.get_barrier_semaphore()
+    for d in range(n):
+        for e in range(n_short):
+            if d or e:
+                pl.semaphore_signal(
+                    barrier, inc=1,
+                    device_id={"wide": peer(d), "short": lax.rem(s + e, n_short)},
+                    device_id_type=MESH,
+                )
+
+    def cols(c):
+        return pl.ds(c * fchunk, fchunk)
+
+    fgu = []
+    for c in range(n_chunk):
+        fgu.append((fetch(gate.at[:, cols(c)], g_v.at[c]), fetch(up.at[:, cols(c)], u_v.at[c])))
+        if c == 0:
+            fkv = [fetch(keys, k_v), fetch(values, v_v), fetch(state, s_v)]
+    fmo = [fetch(mixer_out.at[g], m_v.at[g, pl.ds(0, ocol)]) for g in range(n_short)]
+    fdn = [fetch(down.at[:, pl.ds(o * ochunk, ochunk)], d_v.at[o]) for o in range(n_oc)]
+
+    pl.semaphore_wait(barrier, n * n_short - 1)
+
+    def remote(src, dst, send, recv, wide, short):
+        copy = pltpu.make_async_remote_copy(
+            src_ref=src, dst_ref=dst, send_sem=send, recv_sem=recv,
+            device_id={"wide": wide, "short": short}, device_id_type=MESH,
+        )
+        copy.start()
+        return copy
+
+    def arrived(buf, recv):
+        pltpu.make_async_copy(buf, buf, recv).wait()
+
+    sent = []
+
+    for d in range(1, n):
+        sent.append(remote(tokens, xg.at[me], sem_gs.at[d], sem_gr.at[me], peer(d), s))
+    own_tokens = pltpu.make_async_copy(tokens, xg.at[me], sem_loc.at[0])
+    own_tokens.start()
+    for g in range(n_short):
+        if opad > ocol:
+            m_v[g, ocol:opad, :] = jnp.zeros((opad - ocol, width), BF16)
+    feat[...] = jnp.zeros_like(feat)
+    bc[...] = jnp.zeros_like(bc)
+    qbuf[...] = jnp.zeros_like(qbuf)
+    knbuf[...] = jnp.zeros_like(knbuf)
+    vnbuf[...] = jnp.zeros_like(vnbuf)
+    cbuf[...] = jnp.zeros_like(cbuf)
+    c_b[...] = jnp.zeros_like(c_b)
+    tot[...] = jnp.zeros_like(tot)
+    own[...] = jnp.zeros_like(own)
+    own_tokens.wait()
+    for d in range(1, n):
+        arrived(xg.at[peer(d)], sem_gr.at[peer(d)])
+    for j in range(n):
+        xf[rows * j : rows * (j + 1), :] = xg[j].astype(F32)
+    x = xf[...]
+    sq_send[...] = jnp.broadcast_to(jnp.sum(x * x, axis=1, keepdims=True), sq_send.shape)
+    sent.append(remote(sq_send, sq_recv, sem_ps.at[0], sem_pr.at[0], me, other))
+    xb[...] = (x * gain[...]).astype(BF16)
+
+    for copy in fa:
+        copy.wait()
+    p_send[...] = dot_nt(xb[...], w_a[...])
+    sent.append(remote(p_send, p_recv, sem_ps.at[1], sem_pr.at[1], me, other))
+    fb[0].wait()
+    c_b[:, :gcol] = dot_nt(xb[...], w_b[...])
+    lane = lax.broadcasted_iota(jnp.int32, (total_rows, acol), 1)
+    mine = jnp.where(lane < gcol, c_b[:, :acol], p_send[...])
+    arrived(sq_recv, sem_pr.at[0])
+    mean_square = (sq_send[:, :1] + sq_recv[:, :1]) / D
+    inv = lax.rsqrt(mean_square + epsilon)
+    arrived(p_recv, sem_pr.at[1])
+    tot[:, :acol] = (mine + p_recv[...]) * inv
+    whole = tot[...]
+    wide_lane = lax.broadcasted_iota(jnp.int32, whole.shape, 1)
+    span = whole.shape[1]
+    features = pltpu.roll(
+        jnp.where(wide_lane < gcol, whole, 0.0), lax.rem(me * gcol, LANE), 1
+    )
+    low = pltpu.roll(whole, span - gcol, 1)[:, :LANE]
+    low_lane = lax.broadcasted_iota(jnp.int32, low.shape, 1)
+    low = pltpu.roll(jnp.where(low_lane < scol, low, 0.0), lax.rem(me * scol, LANE), 1)
+    step_all = pltpu.roll(whole, span - gcol - scol, 1)[:, :LANE]
+    step_f[...] = pltpu.roll(step_all, lax.rem(LANE - s * m_heads, LANE), 1)
+    tot[...] = features
+    c_b[:, :LANE] = low
+    for r in range(n):
+        f_send[r, :, :fpad] = tot[rows * r : rows * (r + 1), :].astype(BF16)
+        f_send[r, :, fpad:] = c_b[rows * r : rows * (r + 1), :LANE].astype(BF16)
+    for d in range(1, n):
+        to = peer(d)
+        sent.append(remote(f_send.at[to], f_recv.at[me], sem_fs.at[d], sem_fr.at[me], to, s))
+    own_f = pltpu.make_async_copy(f_send.at[me], f_recv.at[me], sem_loc.at[1])
+    own_f.start()
+
+    half = total_rows // n_short
+
+    def gate_up(c):
+        fgu[c][0].wait()
+        for i in range(n_short):
+            pass
+        both = [dot(xb[...], g_v[c])]
+        fgu[c][1].wait()
+        both.append(dot(xb[...], u_v[c]))
+        for k in range(2):
+            for i in range(n_short):
+                gsc[c, k, i] = both[k][half * i : half * (i + 1)] * inv[half * i : half * (i + 1)]
+        for k in range(2):
+            gu_send[c, k] = gsc[c, k, other].astype(BF16)
+        sent.append(remote(gu_send.at[c], gu_recv.at[c], sem_us.at[c], sem_ur.at[c], me, other))
+
+    def hidden(c):
+        arrived(gu_recv.at[c], sem_ur.at[c])
+        a = gsc[c, 0, s] + gu_recv[c, 0].astype(F32)
+        b = gsc[c, 1, s] + gu_recv[c, 1].astype(F32)
+        hbuf[c, s] = (silu(a) * b).astype(BF16)
+        sent.append(
+            remote(hbuf.at[c, s], hbuf.at[c, s], sem_hs.at[c], sem_hr.at[c], me, other)
+        )
+
+    gate_up(0)
+
+    own_f.wait()
+    for d in range(1, n):
+        arrived(f_recv.at[peer(d)], sem_fr.at[peer(d)])
+    fwidth = feat.shape[1]
+    for j in range(n):
+        base = gcol * j // LANE * LANE
+        w = min(fpad, fwidth - base)
+        feat[:, base : base + w] += f_recv[j, :, :w].astype(F32)
+        base = scol * j // LANE * LANE
+        bc[:, base : base + LANE] += f_recv[j, :, fpad:].astype(F32)
+    for copy in fkv:
+        copy.wait()
+    k_at = q_heads * HEAD_SIZE
+    v_at = k_at + kv_heads * HEAD_SIZE
+    x_at = v_at + kv_heads * HEAD_SIZE
+    z_at = x_at + m_heads * MP
+    cos_t = cosf[...]
+    sin_t = sinf[...]
+
+    def turn(v):
+        return v * cos_t + jnp.concatenate([v[:, HEAD_SIZE // 2 :], v[:, : HEAD_SIZE // 2]], axis=1) * sin_t
+
+    length = lengths[0]
+    for kv in range(kv_heads):
+        for i in range(rep):
+            h = kv * rep + i
+            qbuf[kv, rows * i : rows * (i + 1), :] = turn(feat[:, h * HEAD_SIZE : (h + 1) * HEAD_SIZE])
+        knbuf[kv, :rows, :] = turn(feat[:, k_at + kv * HEAD_SIZE : k_at + (kv + 1) * HEAD_SIZE])
+        vnbuf[kv, :rows, :] = feat[:, v_at + kv * HEAD_SIZE : v_at + (kv + 1) * HEAD_SIZE]
+        head = slice(kv * HEAD_SIZE, (kv + 1) * HEAD_SIZE)
+        query = qbuf[kv].astype(BF16)
+        scale = HEAD_SIZE ** (-0.5)
+        old = dot_nt(query, k_v[:, head]) * scale
+        new = dot_nt(query, knbuf[kv].astype(BF16)) * scale
+        slot = lax.broadcasted_iota(jnp.int32, old.shape, 1)
+        old = jnp.where(slot < length, old, -1e30)
+        token = lax.rem(lax.broadcasted_iota(jnp.int32, new.shape, 0), rows)
+        fresh = lax.broadcasted_iota(jnp.int32, new.shape, 1)
+        new = jnp.where(fresh <= token, new, -1e30)
+        top = jnp.maximum(
+            jnp.max(old, axis=1, keepdims=True), jnp.max(new, axis=1, keepdims=True)
+        )
+        old = jnp.exp(old - top)
+        new = jnp.exp(new - top)
+        den = jnp.sum(old, axis=1, keepdims=True) + jnp.sum(new, axis=1, keepdims=True)
+        obuf[kv] = dot((old / den).astype(BF16), v_v[:, head]) + dot(
+            (new / den).astype(BF16), vnbuf[kv].astype(BF16)
+        )
+        for i in range(rep):
+            h = kv * rep + i
+            own[:, h * HEAD_SIZE : (h + 1) * HEAD_SIZE] = obuf[kv, rows * i : rows * (i + 1), :]
+
+    write = silu(bc[:, :NS])
+    read = silu(bc[:, NS:])
+    rest = read
+    for i in range(3):
+        piece = rest.astype(BF16).astype(F32)
+        cbuf[rows * i : rows * (i + 1), :] = piece
+        rest = rest - piece
+    rbuf[...] = dot_nt(cbuf[...].astype(BF16), s_v[...])
+    carried = rbuf[:rows] + rbuf[rows : 2 * rows] + rbuf[2 * rows : 3 * rows]
+    raw = step_f[pl.ds(rows * me, rows), :][:, :m_heads] + bias[...]
+    step = jnp.maximum(raw, 0.0) + jnp.log1p(jnp.exp(-jnp.abs(raw)))
+    run = [step[:1]]
+    for t in range(1, rows):
+        run.append(run[-1] + step[t : t + 1])
+    age = jnp.concatenate(run, axis=0) * rate[...]
+    kept = jnp.exp(-age)
+    tid = lax.broadcasted_iota(jnp.int32, age.shape, 0)
+    mix = []
+    for u in range(rows):
+        overlap = jnp.sum(read * write[u : u + 1], axis=1, keepdims=True)
+        fade = jnp.exp(-jnp.maximum(age - age[u : u + 1], 0.0))
+        mix.append(jnp.where(tid >= u, fade, 0.0) * step[u : u + 1] * overlap)
+    skips = skip[...]
+    for h in range(m_heads):
+        hs = slice(h * MP, (h + 1) * MP)
+        active = silu(feat[:, x_at + h * MP : x_at + (h + 1) * MP])
+        y = kept[:, h : h + 1] * carried[:, hs] + skips[:, h : h + 1] * active
+        for u in range(rows):
+            y = y + mix[u][:, h : h + 1] * active[u : u + 1]
+        y = y * silu(feat[:, z_at + h * MP : z_at + (h + 1) * MP])
+        ms = jnp.mean(y * y, axis=1, keepdims=True)
+        at = (q_heads + h) * MP
+        own[:, at : at + MP] = y * lax.rsqrt(ms + epsilon) * mixer_gain[:, hs]
+
+    window = opad + LANE
+    for j in range(n):
+        base = ocol * j // LANE * LANE
+        off = ocol * j - base
+        v = own[:, base : base + window]
+        if off:
+            v = jnp.concatenate([v[:, off:], v[:, :off]], axis=1)
+        m_send[j] = v[:, :opad].astype(BF16)
+    for d in range(n):
+        to = peer(d)
+        for e in range(n_short):
+            if d or e:
+                sent.append(
+                    remote(
+                        m_send.at[to], m_recv.at[s, me], sem_ms.at[d, e], sem_mr.at[s, me],
+                        to, lax.rem(s + e, n_short),
+                    )
+                )
+    own_m = pltpu.make_async_copy(m_send.at[me], m_recv.at[s, me], sem_loc.at[2])
+    own_m.start()
+
+    hidden(0)
+    for c in range(1, n_chunk):
+        gate_up(c)
+        if c > 1:
+            hidden(c - 1)
+    own_m.wait()
+    for d in range(n):
+        for e in range(n_short):
+            if d or e:
+                g = lax.rem(s + e, n_short)
+                arrived(m_recv.at[g, peer(d)], sem_mr.at[g, peer(d)])
+    for g in range(n_short):
+        for j in range(n):
+            lhs[g, rows * j : rows * (j + 1), :] = m_recv[g, j].astype(F32)
+    if n_chunk > 1:
+        hidden(n_chunk - 1)
+    for copy in fmo:
+        copy.wait()
+    for c in range(n_chunk):
+        arrived(hbuf.at[c, other], sem_hr.at[c])
+    for o in range(n_oc):
+        oc = slice(o * ochunk, (o + 1) * ochunk)
+        acc = dot(lhs[0].astype(BF16), m_v[0, :, oc])
+        for g in range(1, n_short):
+            acc = acc + dot(lhs[g].astype(BF16), m_v[g, :, oc])
+        fdn[o].wait()
+        for c in range(n_chunk):
+            acc = acc + dot(
+                hbuf[c].reshape(total_rows, fchunk), d_v[o, c * fchunk : (c + 1) * fchunk, :]
+            )
+        xf[:, oc] = acc
+        for r in range(n):
+            o_send[o, r] = xf[rows * r : rows * (r + 1), oc].astype(BF16)
+        for d in range(1, n):
+            to = peer(d)
+            sent.append(
+                remote(
+                    o_send.at[o, to], o_recv.at[o, me], sem_os.at[o, d], sem_or.at[o, me], to, s
+                )
+            )
+    for o in range(n_oc):
+        oc = slice(o * ochunk, (o + 1) * ochunk)
+        acc = tokens[:, oc].astype(F32) + o_send[o, me].astype(F32)
+        for d in range(1, n):
+            arrived(o_recv.at[o, peer(d)], sem_or.at[o, peer(d)])
+            acc = acc + o_recv[o, peer(d)].astype(F32)
+        out[:, oc] = acc.astype(BF16)
+    for copy in sent:
+        copy.wait_send()
+
+
+def round_up(v):
+    return -(-v // LANE) * LANE
+
+
+def xpad(gcol):
+    return round_up(gcol + LANE - 1)
+
+
+def pieces_of(width, most):
+    tiles = width // LANE
+    for k in range(most, 0, -1):
+        if tiles % k == 0:
+            return k
+    return 1
+
+
+def fused(*args):
+    (tokens, norm_gain, mixer_in, shared_in, step_in, step_bias, decay_rate, skip_gain,
+     cached_keys, cached_values, lengths, state_cache, mixer_gain, mixer_out,
+     gate_weight, up_weight, down_weight) = args
+    n = lax.axis_size("wide")
+    n_short = lax.axis_size("short")
+    rows, width = tokens.shape
+    gcol = mixer_in.shape[2]
+    scol = shared_in.shape[1]
+    ncol = step_in.shape[1]
+    ocol = mixer_out.shape[1]
+    ffl = gate_weight.shape[1]
+    n_chunk = pieces_of(ffl, 3)
+    fchunk = ffl // n_chunk
+    n_oc = pieces_of(width, 4)
+    ochunk = width // n_oc
+    m_heads = MH // n_short
+    kv_heads = KEY_VALUE_HEADS // n_short
+    total_rows = n * rows
+    acol = gcol + scol + ncol
+    fpad = xpad(gcol)
+    opad = round_up(ocol)
+    features = n * gcol
+    outs = n * ocol
+    half = total_rows // n_short
+    positions = lengths + jnp.arange(rows, dtype=jnp.int32)
+    cos_table, sin_table = rope_tables(positions)
+    cosf = jnp.concatenate([cos_table, cos_table], axis=-1)
+    sinf = jnp.concatenate([-sin_table, sin_table], axis=-1)
+    dims = (n, n_short, rows, width, gcol, scol, ncol, ocol, n_chunk, fchunk, n_oc, ochunk)
+    vm = pl.BlockSpec(memory_space=pltpu.VMEM)
+    sm = pl.BlockSpec(memory_space=pltpu.SMEM)
+    hb = pl.BlockSpec(memory_space=pl.ANY)
+    V = pltpu.VMEM
+    dma = pltpu.SemaphoreType.DMA
+    kvw = cached_keys.shape[2]
+    slots = cached_keys.shape[1]
+    scratch = [
+        V((acol, width), BF16), V((gcol, width), BF16), V((slots, kvw), BF16),
+        V((slots, kvw), BF16), V((m_heads * MP, NS), BF16),
+        V((n_chunk, width, fchunk), BF16), V((n_chunk, width, fchunk), BF16),
+        V((n_short, opad, width), BF16), V((n_oc, ffl, ochunk), BF16),
+        V((n, rows, width), BF16), V((total_rows, width), F32), V((total_rows, width), BF16),
+        V((total_rows, LANE), F32), V((total_rows, LANE), F32),
+        V((total_rows, acol), F32), V((total_rows, acol), F32), V((total_rows, fpad), F32),
+        V((total_rows, fpad), F32), V((total_rows, LANE), F32),
+        V((n, rows, fpad + LANE), BF16), V((n, rows, fpad + LANE), BF16),
+        V((rows, features), F32), V((rows, 2 * NS), F32),
+        V((kv_heads, 32, HEAD_SIZE), F32), V((kv_heads, 16, HEAD_SIZE), F32),
+        V((kv_heads, 16, HEAD_SIZE), F32), V((kv_heads, 32, HEAD_SIZE), F32),
+        V((16, NS), F32), V((16, m_heads * MP), F32),
+        V((rows, round_up(outs) + opad + LANE), F32),
+        V((n, rows, opad), BF16), V((n_short, n, rows, opad), BF16),
+        V((n_short, total_rows, opad), F32),
+        V((n_chunk, 2, n_short, half, fchunk), F32),
+        V((n_chunk, 2, half, fchunk), BF16), V((n_chunk, 2, half, fchunk), BF16),
+        V((n_chunk, n_short, half, fchunk), BF16),
+        V((n_oc, n, rows, ochunk), BF16), V((n_oc, n, rows, ochunk), BF16),
+        dma((4 + 2 * n_chunk + 3 + n_short + n_oc,)), dma((3,)),
+        dma((n,)), dma((n,)), dma((2,)), dma((2,)), dma((n,)), dma((n,)),
+        dma((n, n_short)), dma((n_short, n)), dma((n_chunk,)), dma((n_chunk,)),
+        dma((n_chunk,)), dma((n_chunk,)), dma((n_oc, n)), dma((n_oc, n)),
+    ]
+    return pl.pallas_call(
+        functools.partial(fused_kernel, dims),
+        out_shape=jax.ShapeDtypeStruct((rows, width), BF16),
+        in_specs=[vm, vm, vm, vm, vm, sm, vm, vm, vm] + [hb] * 10,
+        out_specs=vm,
+        scratch_shapes=scratch,
+        name="layer",
+        compiler_params=pltpu.CompilerParams(
+            collective_id=0, has_side_effects=True, vmem_limit_bytes=66 * 1000 * 1000
+        ),
+    )(
+        tokens, norm_gain[None, :], step_bias[None, :], decay_rate[None, :], skip_gain[None, :],
+        lengths, cosf, sinf, mixer_gain[None, :],
+        jnp.transpose(mixer_in, (1, 2, 0)), shared_in.T, step_in.T,
+        cached_keys[0], cached_values[0], state_cache.reshape(m_heads * MP, NS),
+        mixer_out, gate_weight, up_weight, down_weight,
+    )
+
+
+def fits(n, n_short, args):
+    tokens, mixer_in, shared_in, step_in = args[0], args[2], args[3], args[4]
+    return (
+        n_short == 2
+        and tokens.shape[0] == DRAFT_TOKENS
+        and n * DRAFT_TOKENS == 32
+        and mixer_in.shape[2] % 16 == 0
+        and shared_in.shape[1] % 16 == 0
+        and LANE % shared_in.shape[1] == 0
+        and step_in.shape[1] % 16 == 0
+        and args[13].shape[1] % 16 == 0
+        and args[14].shape[1] % LANE == 0
+    )
+
+
+def layer(*args):
+    if fits(lax.axis_size("wide"), lax.axis_size("short"), args):
+        return fused(*args)
+    return on_device(*args)
+
+
 def solution(mesh):
     in_specs = (
         P(("groups", "wide"), "short"),
@@ -241,5 +707,5 @@
     )
     out_specs = P(("groups", "wide"), "short")
     return jax.shard_map(
-        on_device, mesh=mesh, in_specs=in_specs, out_specs=out_specs, check_vma=False
-    )
+        layer, mesh=mesh, in_specs=in_specs, out_specs=out_specs, check_vma=False
+    )

time: 177 us -> 41.7 us (0.24)
  blocking collectives: 53.5 us -> 0 us
  matrix products: 45.4 us -> 0 us
  Pallas kernels: 0 us -> 37.4 us
  other arithmetic: 24.1 us -> 0.78 us
  starting transfers between devices: 15 us -> 0 us
  between operations: 14.2 us -> 0.67 us
  local copies, waits for them, and re-layouts: 13.2 us -> 2.65 us
  waiting for transfers between devices: 10.4 us -> 0 us
    dot_general x14 -> x0, matrix products: 43.6 us -> none  [the longest x4 10.6 us: scan_one(): jnp.einsum('hpn,n->hp', hstate, read_vec[draft_index], precision=lax.Prec...]
    pallas_call x0 -> x1, Pallas kernels: none -> 37.4 us  [fused(): pl.pallas_call(functools.partial(fused_kernel, dims), out_shape=jax.Shape...]
    all_gather x3 -> x0, blocking collectives: 36.2 us -> none  [the longest x1 32.2 us: on_device(): gathered = lax.all_gather(normed, 'wide', axis=0, tiled=True)]
    unnamed x3 -> x0, other arithmetic: 19.2 us -> none
    all_to_all x3 -> x0, starting transfers between devices: 14.9 us -> none  [the longest x1 6.12 us: on_device(): lax.all_to_all(group_part, 'wide', split_axis=0, concat_axis=2, tiled=True)]
    all_to_all x1 -> x0, blocking collectives: 10.5 us -> none  [on_device(): lax.all_to_all(summed.reshape(n_wide, local_rows, width_half).astype(jnp....]
    all_to_all x3 -> x0, waiting for transfers between devices: 10.3 us -> none  [the longest x1 6.92 us: on_device(): lax.all_to_all(group_part, 'wide', split_axis=0, concat_axis=2, tiled=True)]
    unnamed x30 -> x1, local copies, waits for them, and re-layouts: 6.24 us -> 1.34 us
  transfers between devices with their start and end apart: 6 -> 0, of which waited for: 2 -> 0; matrix products, arithmetic and copies ran while one was open for 36% -> 0% of each run, Pallas kernels for 0% -> 0%
where the time goes in v1:
time: 41.7 us; the launch traced here: 41.5 us
  Pallas kernels  37.4 us (90%)
  local copies, waits for them, and re-layouts  2.65 us (6%)
  other arithmetic  0.78 us (2%)
  between operations  0.67 us (2%)
    pallas_call x1, Pallas kernels, fused(): pl.pallas_call(functools.partial(fused_kernel, dims), out_shape=jax.Shape...  37.4 us
    unnamed x1, local copies, waits for them, and re-layouts  1.34 us
    broadcast_in_dim x1, local copies, waits for them, and re-layouts, fused(): norm_gain[None, :]  1.31 us

profile of v1, /device:TPU:0, one launch (start us, length us, event | category | flops | bytes accessed | tf_op | source)
XLA Modules:
  0.0 41.5 jit_solution(6570098755225208393)
XLA Ops:
  0.7 0.1 fusion
  0.8 0.7 %pad_maximum_fusion = (f32[4,128]{1,0:T(4,128)}, f32[4,128]{1,0:T(4,128)}) fusion(f32[4,64]{1,0:T(4,128)S(1)} %get-tuple-element.7, f32[4,64]{1,0:T(4,128)S(1)} %get-tuple-element.6, f32[4,64]{1,0:T(4,128)S(1)} %get-tuple-element.5), kind=kLoop, calls=%fused_computation.2 | loop fusion | flops 1024 | bytes 7168 | tf_op jit(solution)/shard_map/concatenate | solution.py:612
  1.5 1.3 %broadcast_in_dim.17.gain = f32[1,2560]{1,0:T(1,128)} reshape(f32[2560]{0:T(1024)} %param.18) | data formatting | bytes 20480 | tf_op jit(solution)/shard_map/broadcast_in_dim | solution.py:659
  2.8 37.4 %layer.1 = bf16[4,2560]{1,0:T(4,128)(2,1)} custom-call(bf16[4,2560]{1,0:T(4,128)(2,1)} %tokens.1, f32[1,2560]{1,0:T(1,128)} %broadcast_in_dim.17.gain, f32[1,16]{1,0:T(1,128)} %bitcast.19, f32[1,16]{1,0:T(1,128)} %bitcast.20, f32[1,16]{1,0:T(1,128)} %bitcast.21, s32[1]{0:T(128)} %copy.19.lengths, f32[4,128]{1,0:T(4,128)} %get-tuple-element.8.cosf, ...), custom_call_target="tpu_custom_call" | custom-call | tf_op jit(solution)/shard_map/layer/pallas_call | solution.py:648
  40.1 1.3 %copy.20 = bf16[4,2560]{1,0:T(4,128)(2,1)} copy(bf16[4,2560]{1,0:T(4,128)(2,1)} %layer.1) | data formatting | bytes 40960
  (2 shorter events, 0.0 us)
